TPU v7x, 128 devices: a whole 4x4x4 slice. The times are simulated.
128 devices in a mesh: lat: 16 (over x_lo, z, core), lon: 8 (over y, x_hi).
Axes of the slice: x: 4 (x_hi: 2, x_lo: 2; x = x_hi * 2 + x_lo), y: 4, z: 4, core: 2. Of those that a mesh axis runs over, the one named last changes fastest.
Arguments:
- forcing: float32 [16, 2048, 2048], P(None, 'lat', 'lon'), may hold values from -6 to 6
- metric_lon: float32 [2048, 2048], P('lat', 'lon'), may hold values from -0.5 to 0.5
- metric_lat: float32 [2048, 2048], P('lat', 'lon'), may hold values from -0.5 to 0.5
- lon_weights: float32 [2048], P('lon'), may hold values from 0.5 to 2
- eigen_basis: float32 [2048, 2048], replicated, may hold values from -0.125 to 0.125
- lower_mult: float32 [16, 2048, 2048], P('lon', 'lat'), may hold values from -1 to 0
- pivot_inverse: float32 [16, 2048, 2048], P('lon', 'lat'), may hold values from 0 to 2
- upper_coef: float32 [16, 2048, 2048], P('lon', 'lat'), may hold values from -33554432 to 0
Outputs:
- solution: float32 [16, 2048, 2048], P(None, 'lat', 'lon')
All inputs are finite; a program needn't handle non-finite values.
Results may differ from a plain program's by a relative error of at most 0.000082.
Values sent between devices are 32-bit elements; how exact they have to be, the bound alone decides.
A program may use at most 128 MiB of HBM per device.

v0:
```python
import jax
import jax.numpy as jnp
from jax import lax
from jax.sharding import PartitionSpec as P


def padded(shard, sides, width, wrap):
    for axis, dim in sides:
        count, length = (lax.axis_size(axis), shard.shape[dim])
        up = [(i, (i + 1) % count) for i in range(count if wrap else count - 1)]
        down = [(j, i) for i, j in up]
        last = lax.slice_in_dim(shard, length - width, length, axis=dim)
        initial = lax.slice_in_dim(shard, 0, width, axis=dim)
        before = lax.ppermute(last, axis, up)
        after = lax.ppermute(initial, axis, down)
        shard = jnp.concatenate([before, shard, after], axis=dim)
    return shard


def copy_for_each(shard, axis):
    count = lax.axis_size(axis)
    return lax.all_to_all(
        jnp.broadcast_to(shard[None], (count, *shard.shape)), axis, 0, 0, tiled=True
    )


def gathered_once(shard, axis):
    leaves = jax.tree.leaves(shard)
    sequence = sorted(range(len(leaves)), key=lambda k: -leaves[k].size)
    width = (1, *leaves[sequence[0]].shape)[-1]
    lines = [
        jnp.pad(leaves[k].reshape(-1), (0, -leaves[k].size % width)).reshape(-1, width)
        for k in sequence
    ]
    both, at, found = (copy_for_each(jnp.concatenate(lines), axis), 0, {})
    for k, line in zip(sequence, lines):
        slab = both[:, at : at + len(line)].reshape(len(both), -1)
        found[k] = slab[:, : leaves[k].size].reshape(-1, *leaves[k].shape)
        at += len(line)
    numbers = iter(range(len(leaves)))
    return jax.tree.map(lambda _: found[next(numbers)], shard)


def folded_in_pairs(pieces, combine):
    while len(jax.tree.leaves(pieces)[0]) > 1:
        pieces = jax.vmap(combine)(
            *(jax.tree.map(lambda part: part[side::2], pieces) for side in (0, 1))
        )
    return jax.tree.map(lambda part: part[0], pieces)


def carried_in(shard, axis, combine, identity):
    count, position = (lax.axis_size(axis), lax.axis_index(axis))
    passed = jnp.arange(count) < position

    def carried_kept(part, zero, own):
        part = jnp.where(
            passed.reshape(-1, *(1 for _ in own.shape)), part, jnp.asarray(zero, own.dtype)
        )
        return part

    pieces = gathered_once(shard, axis)
    return folded_in_pairs(jax.tree.map(carried_kept, pieces, identity, shard), combine)


def collected_alike(shard, axis):
    leaves, found = (jax.tree.leaves(shard), {})
    for initial, a in enumerate(leaves):
        if initial not in found:
            alike = [k for k, b in enumerate(leaves) if b.dtype == a.dtype]
            got = (
                gathered_once([leaves[k] for k in alike], axis)
                if len(alike) > 1
                else [copy_for_each(a, axis)]
            )
            for k, b in zip(alike, got):
                found[k] = b
    numbers = iter(range(len(leaves)))
    return jax.tree.map(lambda _: found[next(numbers)], shard)


def entering_2(shard, axis, combine, identity):
    count, position = (lax.axis_size(axis), lax.axis_index(axis))
    passed = jnp.arange(count) > position

    def entering_kept(part, zero, own):
        part = jnp.where(
            passed.reshape(-1, *(1 for _ in own.shape)), part, jnp.asarray(zero, own.dtype)
        )
        return part[::-1]

    pieces = collected_alike(shard, axis)
    return folded_in_pairs(jax.tree.map(entering_kept, pieces, identity, shard), combine)


def compose(earlier, later):
    return (later[0] * earlier[0], later[0] * earlier[1] + later[1])


def band_recurrence(factor, source, reverse_order):
    modes, rows, columns = factor.shape
    block = min(8, rows)
    groups = rows // block
    factor_blocks = factor.reshape(modes, groups, block, columns)
    source_blocks = source.reshape(modes, groups, block, columns)
    order = list(range(block))
    if reverse_order:
        order = order[::-1]
    running_scale = jnp.ones((modes, groups, columns), jnp.float32)
    running_shift = jnp.zeros((modes, groups, columns), jnp.float32)
    scale_rows = [None] * block
    shift_rows = [None] * block
    for position in order:
        step_factor = factor_blocks[:, :, position, :]
        running_scale = step_factor * running_scale
        running_shift = step_factor * running_shift + source_blocks[:, :, position, :]
        scale_rows[position] = running_scale
        shift_rows[position] = running_shift
    group_order = list(range(groups))
    if reverse_order:
        group_order = group_order[::-1]
    carry_scale = jnp.ones((modes, columns), jnp.float32)
    carry_shift = jnp.zeros((modes, columns), jnp.float32)
    enter_scale = [None] * groups
    enter_shift = [None] * groups
    for group in group_order:
        enter_scale[group] = carry_scale
        enter_shift[group] = carry_shift
        carry_scale, carry_shift = compose(
            (carry_scale, carry_shift), (running_scale[:, group, :], running_shift[:, group, :])
        )
    local_scale = jnp.stack(scale_rows, axis=2)
    local_shift = jnp.stack(shift_rows, axis=2)
    group_scale = jnp.stack(enter_scale, axis=1)[:, :, None, :]
    group_shift = jnp.stack(enter_shift, axis=1)[:, :, None, :]
    full_scale = (local_scale * group_scale).reshape(modes, rows, columns)
    full_shift = (local_shift + local_scale * group_shift).reshape(modes, rows, columns)
    return (full_scale, full_shift, (carry_scale, carry_shift))


def per_device(
    forcing, metric_lon, metric_lat, lon_weights, eigen_basis, lower_mult, pivot_inverse, upper_coef
):
    wrapped = padded(forcing, (("lon", 2),), 1, True)
    stacked = padded(forcing, (("lat", 1),), 1, False)
    source_term = (
        forcing
        + metric_lon * (wrapped[:, :, :-2] + wrapped[:, :, 2:])
        + metric_lat * (stacked[:, :-2, :] + stacked[:, 2:, :])
    )
    weighted = source_term * lon_weights
    spectral = jnp.einsum(
        "kji,im->kjm",
        lax.all_to_all(weighted, "lon", split_axis=0, concat_axis=2, tiled=True),
        eigen_basis,
        precision=lax.Precision.HIGHEST,
    )
    down_scale, down_shift, down_summary = band_recurrence(-lower_mult, spectral, False)
    identity = (jnp.ones_like(down_summary[0]), jnp.zeros_like(down_summary[1]))
    entering = carried_in(down_summary, "lat", compose, identity)[1]
    sweep = down_shift + down_scale * entering[:, None, :]
    up_factor = -(upper_coef * pivot_inverse)
    up_source = pivot_inverse * sweep
    up_scale, up_shift, up_summary = band_recurrence(up_factor, up_source, True)
    identity_up = (jnp.ones_like(up_summary[0]), jnp.zeros_like(up_summary[1]))
    arriving = entering_2(up_summary, "lat", compose, identity_up)[1]
    modal = up_shift + up_scale * arriving[:, None, :]
    on_grid = jnp.einsum("kjm,im->kji", modal, eigen_basis, precision=lax.Precision.HIGHEST)
    return lax.all_to_all(on_grid, "lon", split_axis=2, concat_axis=0, tiled=True)


def solution(mesh):
    placed = (
        P(None, "lat", "lon"),
        P("lat", "lon"),
        P("lat", "lon"),
        P("lon"),
        P(),
        P("lon", "lat", None),
        P("lon", "lat", None),
        P("lon", "lat", None),
    )
    return jax.shard_map(
        per_device, mesh=mesh, in_specs=placed, out_specs=P(None, "lat", "lon"), check_vma=False
    )
```

profile of v0, /device:TPU:1, one launch (start us, length us, event | category | flops | bytes accessed | tf_op | source)
XLA Modules:
  0.0 222.5 jit_solution(854617699514591773)
XLA Ops:
  1.0 4.9 %collective-permute-start.2 = (f32[16,1,256]{2,1,0:T(1,128)S(1)}, f32[16,1,256]{2,1,0:T(1,128)S(1)}, u32[]{:S(2)}, u32[]{:S(2)}) collective-permute-start(f32[16,1,256]{2,1,0:T(1,128)S(1)} %get-tuple-element.92), channel_id=1, source_target_pairs={{0,8},{8,16},{16,24},{24,32},{32,40},{40,48},{48,56},{56,64},{64,7... | collective-permute-start | bytes 49160 | tf_op jit(solution)/shard_map/ppermute | solution.py:14
  7.9 2.9 %fusion.108 = (f32[16,128,1]{2,1,0:T(8,128)}, f32[16,128,1]{2,1,0:T(8,128)S(1)}) fusion(f32[16,128,256]{2,1,0:T(8,128)} %param.8), kind=kLoop, calls=%fused_computation.380 | loop fusion | bytes 32768 | tf_op jit(solution)/shard_map/slice | solution.py:12
  12.5 2.8 %collective-permute-start = (f32[16,128,1]{1,0,2:T(8,128)S(1)}, f32[16,128,1]{1,0,2:T(8,128)S(1)}, u32[]{:S(2)}, u32[]{:S(2)}) collective-permute-start(f32[16,128,1]{1,0,2:T(8,128)S(1)} %copy.151), channel_id=1, source_target_pairs={{0,1},{1,2},{2,3},{3,4},{4,5},{5,6},{6,7},{7,0},{8,9},{9,10},{10,1... | collective-permute-start | bytes 24584 | tf_op jit(solution)/shard_map/ppermute | solution.py:14
  15.6 2.5 %collective-permute-start.1 = (f32[16,128,1]{1,0,2:T(8,128)S(1)}, f32[16,128,1]{1,0,2:T(8,128)S(1)}, u32[]{:S(2)}, u32[]{:S(2)}) collective-permute-start(f32[16,128,1]{1,0,2:T(8,128)S(1)} %copy.152), channel_id=1, source_target_pairs={{1,0},{2,1},{3,2},{4,3},{5,4},{6,5},{7,6},{0,7},{9,8},{10,9},{11,1... | collective-permute-start | bytes 24584 | tf_op jit(solution)/shard_map/ppermute | solution.py:15
  21.0 4.0 %fusion.7 = f32[16,128,256]{2,1,0:T(8,128)} fusion(f32[16,1,256]{2,1,0:T(1,128)S(1)} %collective-permute-done.3, f32[16,128,256]{2,1,0:T(8,128)S(1)} %copy-done.1, f32[16,1,256]{2,1,0:T(1,128)S(1)} %collective-permute-done.2, f32[16,128,1]{2,1,0:T(8,128)} %copy.101, f32[16,128,1]{2,1,0:T(8,128)S(1)} %copy.99, f32[256]{0:T(256)S(1)} %copy-done.22, ...), kind=kLoop, calls=%fused_computation.8 | loop fusion | flops 5767168 | bytes 4506624 | tf_op jit(solution)/shard_map/mul | solution.py:151
  25.0 6.3 %all-to-all-start = ((f32[16,128,256]{2,1,0:T(8,128)}), f32[16,128,256]{2,1,0:T(8,128)S(1)}, u32[]{:S(2)}, u32[]{:S(2)}) async-start(f32[16,128,256]{2,1,0:T(8,128)} %fusion.7), calls=%async_computation | async-start | bytes 4194304 | tf_op jit(solution)/shard_map/all_to_all | solution.py:154
  32.6 3.1 %negate_bitcast_fusion = f32[2,16,8,2048]{3,2,1,0:T(8,128)} fusion(f32[2,128,2048]{2,1,0:T(8,128)} %param.13), kind=kLoop, calls=%fused_computation.27 | loop fusion | flops 524288 | bytes 4194304 | tf_op jit(solution)/shard_map/reshape | solution.py:104
  35.7 24.1 %all-to-all-done = f32[16,128,256]{2,1,0:T(8,128)S(1)} async-done(((f32[16,128,256]{2,1,0:T(8,128)}), f32[16,128,256]{2,1,0:T(8,128)S(1)}, u32[]{:S(2)}, u32[]{:S(2)}) %all-to-all-start) | async-done | bytes 2097184 | tf_op jit(solution)/shard_map/all_to_all | solution.py:154
  59.8 2.5 %copy.532 = f32[8,2,128,256]{3,0,2,1:T(8,128)} copy(f32[8,2,128,256]{3,2,1,0:T(8,128)S(1)} %bitcast.627) | data formatting | bytes 4194304 | tf_op jit(solution)/shard_map/all_to_all | solution.py:154
  64.0 17.1 %fusion = f32[2,16,8,2048]{3,2,1,0:T(8,128)S(1)} fusion(f32[2,16,8,2048]{3,2,1,0:T(8,128)S(1)} %dot_general.8, f32[2048,2048]{1,0:T(8,128)} %param.12), kind=kOutput, calls=%fused_computation | convolution fusion | flops 12884901888 | bytes 20971520 | tf_op jit(solution)/shard_map/kji,im->kjm/dot_general | solution.py:152
  81.2 3.2 %fusion.107 = (f32[2,16,1,2048]{3,2,1,0:T(1,128)S(1)}, f32[2,16,1,2048]{3,2,1,0:T(1,128)S(1)}, f32[2,16,1,2048]{3,2,1,0:T(1,128)S(1)}, f32[2,16,1,2048]{3,2,1,0:...) fusion(f32[2,16,8,2048]{3,2,1,0:T(8,128)S(1)} %fusion, ...), kind=kLoop, calls=%fused_computation.379 | loop fusion | bytes 8388608 | tf_op jit(solution)/shard_map/slice | solution.py:116
  85.7 2.2 fusion.33
  91.1 6.8 %all-to-all-start.1 = ((f32[16,4,2048]{2,1,0:T(4,128)}), f32[16,4,2048]{2,1,0:T(4,128)}, u32[]{:S(2)}, u32[]{:S(2)}) async-start(f32[16,4,2048]{2,1,0:T(4,128)} %broadcast_in_dim.48), calls=%async_computation.1 | async-start | bytes 1048576 | tf_op jit(solution)/shard_map/all_to_all | solution.py:22
  109.0 4.1 %multiply_add_fusion.1 = (f32[8,4,8,2048]{3,0,1,2:T(8,128)S(1)}, f32[8,4,8,2048]{3,0,1,2:T(8,128)}) fusion(f32[8,4,8,2048]{3,0,1,2:T(8,128)} %bitcast.632, f32[8,4,8,2048]{3,0,1,2:T(8,128)} %bitcast.633, f32[8,4,2048]{2,0,1:T(8,128)S(1)} %bitcast.635, f32[8,4,2048]{2,0,1:T(8,128)S(1)} %bitcast.634), kind=kLoop, calls=%fused_computation.26 | loop fusion | flops 1572864 | bytes 8912896 | tf_op jit(solution)/shard_map/add | solution.py:137
  115.1 4.9 %fusion.16 = (f32[2,16,8,2048]{3,2,1,0:T(8,128)S(1)}, f32[2,16,8,2048]{3,2,1,0:T(8,128)S(1)}) fusion(f32[2,128,2048]{2,1,0:T(8,128)} %param.14, f32[2,16,8,2048]{3,0,1,2:T(2,128)S(1)} %bitcast.626, f32[2,16,8,2048]{3,0,1,2:T(2,128)S(1)} %bitcast.625, f32[2,2048]{1,0:T(2,128)S(1)} %fusion.49, f32[2,128,2048]{2,1,0:T(8,128)} %param.15), kind=kLoop, calls=%fused_computation.21 | loop fusion | flops 2621440 | bytes 12599296 | tf_op jit(solution)/shard_map/reshape | solution.py:105
  123.1 2.4 %bitcast_add_fusion.1 = (f32[2,16,2048]{2,0,1:T(2,128)S(1)}, f32[2,16,2048]{2,0,1:T(2,128)S(1)}) fusion(f32[2,16,1,2048]{3,2,1,0:T(1,128)S(1)} %get-tuple-element.75, f32[2,16,1,2048]{3,2,1,0:T(1,128)S(1)} %get-tuple-element.69, f32[2,16,1,2048]{3,2,1,0:T(1,128)S(1)} %get-tuple-element.70, f32[2,16,1,2048]{3,2,1,0:T(1,128)S(1)} %get-tuple-element.71, ...), kind=kLoop, calls=%fused_computation.37 | loop fusion | flops 1507328 | bytes 4718592 | tf_op jit(solution)/shard_map/add | solution.py:116
  125.9 3.7 %add_dynamic-update-slice_fusion = (f32[2,16,8,2048]{3,0,1,2:T(2,128)}, f32[2,16,1,2048]{3,0,1,2:T(2,128)}, f32[2,16,1,2048]{3,0,1,2:T(2,128)S(1)}, f32[2,16,1,2...) fusion(f32[2,16,1,2048]{3,2,1,0:T(1,128)S(1)} %get-tuple-elemen, ...), kind=kLoop, calls=%fused_computation.85 | loop fusion | flops 1507326 | bytes 6029312
  132.4 5.7 %all-to-all-start.2 = ((f32[16,4,2048]{2,1,0:T(4,128)}), f32[16,4,2048]{2,1,0:T(4,128)}, u32[]{:S(2)}, u32[]{:S(2)}) async-start(f32[16,4,2048]{2,1,0:T(4,128)} %broadcast_in_dim.52), calls=%async_computation.2 | async-start | bytes 1048576 | tf_op jit(solution)/shard_map/all_to_all | solution.py:22
  138.1 2.3 %constant_dynamic-update-slice_fusion.52 = (f32[2,16,8,2048]{3,0,1,2:T(2,128)}, f32[2,16,8,2048]{3,0,1,2:T(2,128)}) fusion(f32[2,16,8,2048]{3,0,1,2:T(2,128)} %get-tuple-element.13, f32[2,16,1,2048]{3,2,1,0:T(1,128)S(1)} %get-tuple-element.69, f32[2,16,1,2048]{3,0,1,2:T(2,128)} %get-tuple-element.14, f32[2,16,1,2048]{3,2,1,0:T(1,128)S(1)} %get-tuple-element.107, ...), kind=kLoop, calls=%fused_computation.153 | loop fusion | flops 196608 | bytes 1572864
  150.1 4.2 %multiply_add_fusion = (f32[8,4,8,2048]{3,0,1,2:T(8,128)S(1)}, f32[8,4,8,2048]{3,0,1,2:T(8,128)}) fusion(f32[8,4,8,2048]{3,0,1,2:T(8,128)} %bitcast.630, f32[8,4,8,2048]{3,0,1,2:T(8,128)} %bitcast.631, f32[8,4,2048]{2,0,1:T(8,128)S(1)} %bitcast.636, f32[8,4,2048]{2,0,1:T(8,128)S(1)} %bitcast.637), kind=kLoop, calls=%fused_computation.25 | loop fusion | flops 1572864 | bytes 8912896 | tf_op jit(solution)/shard_map/add | solution.py:137
  156.3 27.4 %fusion.2 = f32[2,128,2048]{2,1,0:T(8,128)} fusion(f32[2048,2048]{1,0:T(8,128)} %param.12, f32[2,16,8,2048]{3,0,1,2:T(2,128)S(1)} %bitcast.624, f32[2,16,8,2048]{3,0,1,2:T(2,128)S(1)} %bitcast.623, f32[2,2048]{1,0:T(2,128)S(1)} %fusion.47), kind=kOutput, calls=%fused_computation.2 | convolution fusion | flops 12885950464 | bytes 23085056 | tf_op jit(solution)/shard_map/kjm,im->kji/dot_general | solution.py:168
  183.7 2.8 %copy.146 = f32[2,128,2048]{1,0,2:T(2,128)S(1)} copy(f32[2,128,2048]{2,1,0:T(8,128)} %fusion.2) | data formatting | bytes 4194304 | tf_op jit(solution)/shard_map/kjm,im->kji/dot_general | solution.py:168
  186.6 31.5 %all_to_all.43 = f32[2,128,2048]{1,0,2:T(2,128)} all-to-all(f32[2,128,2048]{1,0,2:T(2,128)S(1)} %copy.146), channel_id=1, replica_groups=mesh['lat'=16,'lon'=8] {'lon'}, dimensions={2} | all-to-all | bytes 4194304 | tf_op jit(solution)/shard_map/all_to_all | solution.py:169
  218.1 4.1 %copy.147 = f32[8,2,128,256]{3,2,1,0:T(8,128)} copy(f32[8,2,128,256]{2,1,3,0:T(2,128)} %bitcast.629) | data formatting | bytes 4194304 | tf_op jit(solution)/shard_map/all_to_all | solution.py:169
  (160 shorter events, 45.9 us)
Async XLA Ops:
  1.0 20.0 %collective-permute-start.2 = (f32[16,1,256]{2,1,0:T(1,128)S(1)}, f32[16,1,256]{2,1,0:T(1,128)S(1)}, u32[]{:S(2)}, u32[]{:S(2)}) collective-permute-start(f32[16,1,256]{2,1,0:T(1,128)S(1)} %get-tuple-element.92), channel_id=1, source_target_pairs={{0,8},{8,16},{16,24},{24,32},{32,40},{40,48},{48,56},{56,64},{64,7... | collective-permute-start | bytes 49160 | tf_op jit(solution)/shard_map/ppermute | solution.py:14
  5.9 15.0 %collective-permute-start.3 = (f32[16,1,256]{2,1,0:T(1,128)S(1)}, f32[16,1,256]{2,1,0:T(1,128)S(1)}, u32[]{:S(2)}, u32[]{:S(2)}) collective-permute-start(f32[16,1,256]{2,1,0:T(1,128)S(1)} %get-tuple-element.93), channel_id=1, source_target_pairs={{8,0},{16,8},{24,16},{32,24},{40,32},{48,40},{56,48},{64,56},{72,6... | collective-permute-start | bytes 49160 | tf_op jit(solution)/shard_map/ppermute | solution.py:15
  10.7 10.2 %copy-start.1 = (f32[16,128,256]{2,1,0:T(8,128)S(1)}, f32[16,128,256]{2,1,0:T(8,128)}, u32[]{:S(2)}) copy-start(f32[16,128,256]{2,1,0:T(8,128)} %param.8) | copy-start | bytes 6291460
  10.7 10.2 %copy-start.20 = (f32[128,256]{1,0:T(8,128)S(1)}, f32[128,256]{1,0:T(8,128)}, u32[]{:S(2)}) copy-start(f32[128,256]{1,0:T(8,128)} %param.10) | copy-start | bytes 393220
  10.7 10.2 %copy-start.21 = (f32[128,256]{1,0:T(8,128)S(1)}, f32[128,256]{1,0:T(8,128)}, u32[]{:S(2)}) copy-start(f32[128,256]{1,0:T(8,128)} %param.9) | copy-start | bytes 393220
  10.7 10.3 %copy-start.22 = (f32[256]{0:T(256)S(1)}, f32[256]{0:T(256)}, u32[]{:S(2)}) copy-start(f32[256]{0:T(256)} %param.11) | copy-start | bytes 3076
  12.5 6.3 %collective-permute-start = (f32[16,128,1]{1,0,2:T(8,128)S(1)}, f32[16,128,1]{1,0,2:T(8,128)S(1)}, u32[]{:S(2)}, u32[]{:S(2)}) collective-permute-start(f32[16,128,1]{1,0,2:T(8,128)S(1)} %copy.151), channel_id=1, source_target_pairs={{0,1},{1,2},{2,3},{3,4},{4,5},{5,6},{6,7},{7,0},{8,9},{9,10},{10,1... | collective-permute-start | bytes 24584 | tf_op jit(solution)/shard_map/ppermute | solution.py:14
  15.6 4.0 %collective-permute-start.1 = (f32[16,128,1]{1,0,2:T(8,128)S(1)}, f32[16,128,1]{1,0,2:T(8,128)S(1)}, u32[]{:S(2)}, u32[]{:S(2)}) collective-permute-start(f32[16,128,1]{1,0,2:T(8,128)S(1)} %copy.152), channel_id=1, source_target_pairs={{1,0},{2,1},{3,2},{4,3},{5,4},{6,5},{7,6},{0,7},{9,8},{10,9},{11,1... | collective-permute-start | bytes 24584 | tf_op jit(solution)/shard_map/ppermute | solution.py:15
  25.0 34.8 %all-to-all-start = ((f32[16,128,256]{2,1,0:T(8,128)}), f32[16,128,256]{2,1,0:T(8,128)S(1)}, u32[]{:S(2)}, u32[]{:S(2)}) async-start(f32[16,128,256]{2,1,0:T(8,128)} %fusion.7), calls=%async_computation | async-start | bytes 4194304 | tf_op jit(solution)/shard_map/all_to_all | solution.py:154
  64.0 17.2 %copy-start.3 = (f32[2,16,8,2048]{3,2,1,0:T(8,128)S(1)}, f32[2,16,8,2048]{3,2,1,0:T(8,128)}, u32[]{:S(2)}) copy-start(f32[2,16,8,2048]{3,2,1,0:T(8,128)} %negate_bitcast_fusion) | copy-start | bytes 6291460
  84.5 3.4 %copy-start.4 = (f32[2,16,1,2048]{3,2,1,0:T(1,128)}, f32[2,16,1,2048]{3,2,1,0:T(1,128)S(1)}, u32[]{:S(2)}) copy-start(f32[2,16,1,2048]{3,2,1,0:T(1,128)S(1)} %get-tuple-element.189) | copy-start | bytes 786436
  84.5 3.4 %copy-start.6 = (f32[2,16,1,2048]{3,2,1,0:T(1,128)}, f32[2,16,1,2048]{3,2,1,0:T(1,128)S(1)}, u32[]{:S(2)}) copy-start(f32[2,16,1,2048]{3,2,1,0:T(1,128)S(1)} %get-tuple-element.85) | copy-start | bytes 786436
  84.5 3.4 %copy-start.8 = (f32[2,16,1,2048]{3,2,1,0:T(1,128)}, f32[2,16,1,2048]{3,2,1,0:T(1,128)S(1)}, u32[]{:S(2)}) copy-start(f32[2,16,1,2048]{3,2,1,0:T(1,128)S(1)} %get-tuple-element.186) | copy-start | bytes 786436
  85.7 2.8 %copy-start.13 = (f32[2,16,2048]{2,0,1:T(2,128)S(1)}, f32[2,16,2048]{2,0,1:T(2,128)}, u32[]{:S(2)}) copy-start(f32[2,16,2048]{2,0,1:T(2,128)} %constant_dynamic-update-slice_fusion.29) | copy-start | bytes 786436
  91.1 22.0 %all-to-all-start.1 = ((f32[16,4,2048]{2,1,0:T(4,128)}), f32[16,4,2048]{2,1,0:T(4,128)}, u32[]{:S(2)}, u32[]{:S(2)}) async-start(f32[16,4,2048]{2,1,0:T(4,128)} %broadcast_in_dim.48), calls=%async_computation.1 | async-start | bytes 1048576 | tf_op jit(solution)/shard_map/all_to_all | solution.py:22
  97.9 3.2 %copy-start.7 = (f32[2,16,1,2048]{3,2,1,0:T(1,128)S(1)}, f32[2,16,1,2048]{3,2,1,0:T(1,128)}, u32[]{:S(2)}) copy-start(f32[2,16,1,2048]{3,2,1,0:T(1,128)} %copy-done.6) | copy-start | bytes 786436
  97.9 3.1 %copy-start.9 = (f32[2,16,1,2048]{3,2,1,0:T(1,128)S(1)}, f32[2,16,1,2048]{3,2,1,0:T(1,128)}, u32[]{:S(2)}) copy-start(f32[2,16,1,2048]{3,2,1,0:T(1,128)} %copy-done.8) | copy-start | bytes 786436
  104.3 3.1 %copy-start.5 = (f32[2,16,1,2048]{3,2,1,0:T(1,128)S(1)}, f32[2,16,1,2048]{3,2,1,0:T(1,128)}, u32[]{:S(2)}) copy-start(f32[2,16,1,2048]{3,2,1,0:T(1,128)} %copy-done.4) | copy-start | bytes 786436
  106.0 2.9 %copy-start.12 = (f32[2,16,2048]{2,0,1:T(2,128)S(1)}, f32[2,16,2048]{2,0,1:T(2,128)}, u32[]{:S(2)}) copy-start(f32[2,16,2048]{2,0,1:T(2,128)} %copy-done.11) | copy-start | bytes 786436
  106.0 2.9 %copy-start.15 = (f32[2,16,2048]{2,0,1:T(2,128)S(1)}, f32[2,16,2048]{2,0,1:T(2,128)}, u32[]{:S(2)}) copy-start(f32[2,16,2048]{2,0,1:T(2,128)} %copy-done.14) | copy-start | bytes 786436
  132.4 21.9 %all-to-all-start.2 = ((f32[16,4,2048]{2,1,0:T(4,128)}), f32[16,4,2048]{2,1,0:T(4,128)}, u32[]{:S(2)}, u32[]{:S(2)}) async-start(f32[16,4,2048]{2,1,0:T(4,128)} %broadcast_in_dim.52), calls=%async_computation.2 | async-start | bytes 1048576 | tf_op jit(solution)/shard_map/all_to_all | solution.py:22
  145.6 4.5 %copy-start.17 = (f32[2,16,2048]{2,0,1:T(2,128)S(1)}, f32[2,16,2048]{2,0,1:T(2,128)}, u32[]{:S(2)}) copy-start(f32[2,16,2048]{2,0,1:T(2,128)} %copy-done.16) | copy-start | bytes 786436
  145.6 4.5 %copy-start.19 = (f32[2,16,2048]{2,0,1:T(2,128)S(1)}, f32[2,16,2048]{2,0,1:T(2,128)}, u32[]{:S(2)}) copy-start(f32[2,16,2048]{2,0,1:T(2,128)} %copy-done.18) | copy-start | bytes 786436
  154.3 2.1 copy-start
  (6 other events, 6.4 us)
where the time goes:
time: 226 us; the launch traced here: 222 us
  other arithmetic  53.2 us (24%)
  matrix products  44.6 us (20%)
  local copies, waits for them, and re-layouts  36.1 us (16%)
  blocking collectives  31.5 us (14%)
  starting transfers between devices  31 us (14%)
  waiting for transfers between devices  25.3 us (11%)
    all_to_all x1, blocking collectives, per_device(): lax.all_to_all(on_grid, 'lon', split_axis=2, concat_axis=0, tiled=True)  31.5 us
    dot_general x1, matrix products, per_device(): jnp.einsum('kjm,im->kji', modal, eigen_basis, precision=lax.Precision.HIG...  27.4 us
    all_to_all x1, waiting for transfers between devices, per_device(): lax.all_to_all(weighted, 'lon', split_axis=0, concat_axis=2, tiled=True)  24.1 us
    unnamed x49, other arithmetic  20.7 us
    dot_general x1, matrix products, per_device(): jnp.einsum('kji,im->kjm', lax.all_to_all(weighted, 'lon', split_axis=0, c...  17.1 us
    all_to_all x2, starting transfers between devices, copy_for_each(): lax.all_to_all(jnp.broadcast_to(shard[None], (count, *shard.shape)), axis...  12.5 us
    unnamed x69, local copies, waits for them, and re-layouts  10.1 us
    add x2, other arithmetic, band_recurrence(): local_shift + local_scale * group_shift  8.31 us
  transfers between devices with their start and end apart: 7, of which 3 were waited for; matrix products, arithmetic and copies ran while one was open for 19% of the time, Pallas kernels for 0%

commit v1 on v0

--- a/solution.py
+++ b/solution.py
@@ -166,7 +166,10 @@
     arriving = entering_2(up_summary, "lat", compose, identity_up)[1]
     modal = up_shift + up_scale * arriving[:, None, :]
     on_grid = jnp.einsum("kjm,im->kji", modal, eigen_basis, precision=lax.Precision.HIGHEST)
-    return lax.all_to_all(on_grid, "lon", split_axis=2, concat_axis=0, tiled=True)
+    return jnp.concatenate(
+        lax.all_to_all(jnp.stack(jnp.split(on_grid, lax.axis_size("lon"), axis=2)), "lon", 0, 0),
+        axis=0,
+    )
 
 
 def solution(mesh):

time: 226 us -> 219 us (0.969)
  local copies, waits for them, and re-layouts: 36.1 us -> 30.6 us
    all_to_all x1 -> x0, local copies, waits for them, and re-layouts: 4.11 us -> none  [per_device(): lax.all_to_all(on_grid, 'lon', split_axis=2, concat_axis=0, tiled=True)]
    dot_general x1 -> x0, local copies, waits for them, and re-layouts: 2.85 us -> none  [per_device(): jnp.einsum('kjm,im->kji', modal, eigen_basis, precision=lax.Precision.HIG...]
    unnamed x69 -> x77, local copies, waits for them, and re-layouts: 10.1 us -> 11.5 us
  transfers between devices with their start and end apart: 7 -> 7, of which waited for: 3 -> 3; matrix products, arithmetic and copies ran while one was open for 19% -> 20% of each run, Pallas kernels for 0% -> 0%
where the time goes in v1:
time: 219 us; the launch traced here: 216 us
  other arithmetic  53.2 us (24%)
  matrix products  43.8 us (20%)
  starting transfers between devices  31 us (14%)
  blocking collectives  30.9 us (14%)
  local copies, waits for them, and re-layouts  30.6 us (14%)
  waiting for transfers between devices  25.3 us (12%)
    all_to_all x1, blocking collectives, per_device(): lax.all_to_all(jnp.stack(jnp.split(on_grid, lax.axis_size('lon'), axis=2)...  30.9 us
    dot_general x1, matrix products, per_device(): jnp.einsum('kjm,im->kji', modal, eigen_basis, precision=lax.Precision.HIG...  26.6 us
    all_to_all x1, waiting for transfers between devices, per_device(): lax.all_to_all(weighted, 'lon', split_axis=0, concat_axis=2, tiled=True)  24.1 us
    unnamed x49, other arithmetic  20.7 us
    dot_general x1, matrix products, per_device(): jnp.einsum('kji,im->kjm', lax.all_to_all(weighted, 'lon', split_axis=0, c...  17.1 us
    all_to_all x2, starting transfers between devices, copy_for_each(): lax.all_to_all(jnp.broadcast_to(shard[None], (count, *shard.shape)), axis...  12.5 us
    unnamed x77, local copies, waits for them, and re-layouts  11.5 us
    add x2, other arithmetic, band_recurrence(): local_shift + local_scale * group_shift  8.31 us
  transfers between devices with their start and end apart: 7, of which 3 were waited for; matrix products, arithmetic and copies ran while one was open for 20% of the time, Pallas kernels for 0%

profile of v1, /device:TPU:1, one launch (start us, length us, event | category | flops | bytes accessed | tf_op | source)
XLA Modules:
  0.0 215.6 jit_solution(16266097610069696577)
XLA Ops:
  1.0 4.9 %collective-permute-start.2 = (f32[16,1,256]{2,1,0:T(1,128)S(1)}, f32[16,1,256]{2,1,0:T(1,128)S(1)}, u32[]{:S(2)}, u32[]{:S(2)}) collective-permute-start(f32[16,1,256]{2,1,0:T(1,128)S(1)} %get-tuple-element.92), channel_id=1, source_target_pairs={{0,8},{8,16},{16,24},{24,32},{32,40},{40,48},{48,56},{56,64},{64,7... | collective-permute-start | bytes 49160 | tf_op jit(solution)/shard_map/ppermute | solution.py:14
  5.9 1.9 collective-permute-start.3
  7.9 2.9 %fusion.116 = (f32[16,128,1]{2,1,0:T(8,128)}, f32[16,128,1]{2,1,0:T(8,128)S(1)}) fusion(f32[16,128,256]{2,1,0:T(8,128)} %param.8), kind=kLoop, calls=%fused_computation.396 | loop fusion | bytes 32768 | tf_op jit(solution)/shard_map/slice | solution.py:12
  12.5 2.8 %collective-permute-start = (f32[16,128,1]{1,0,2:T(8,128)S(1)}, f32[16,128,1]{1,0,2:T(8,128)S(1)}, u32[]{:S(2)}, u32[]{:S(2)}) collective-permute-start(f32[16,128,1]{1,0,2:T(8,128)S(1)} %copy.147), channel_id=1, source_target_pairs={{0,1},{1,2},{2,3},{3,4},{4,5},{5,6},{6,7},{7,0},{8,9},{9,10},{10,1... | collective-permute-start | bytes 24584 | tf_op jit(solution)/shard_map/ppermute | solution.py:14
  15.6 2.5 %collective-permute-start.1 = (f32[16,128,1]{1,0,2:T(8,128)S(1)}, f32[16,128,1]{1,0,2:T(8,128)S(1)}, u32[]{:S(2)}, u32[]{:S(2)}) collective-permute-start(f32[16,128,1]{1,0,2:T(8,128)S(1)} %copy.148), channel_id=1, source_target_pairs={{1,0},{2,1},{3,2},{4,3},{5,4},{6,5},{7,6},{0,7},{9,8},{10,9},{11,1... | collective-permute-start | bytes 24584 | tf_op jit(solution)/shard_map/ppermute | solution.py:15
  21.0 4.0 %fusion.7 = f32[16,128,256]{2,1,0:T(8,128)} fusion(f32[16,1,256]{2,1,0:T(1,128)S(1)} %collective-permute-done.3, f32[16,128,256]{2,1,0:T(8,128)S(1)} %copy-done.1, f32[16,1,256]{2,1,0:T(1,128)S(1)} %collective-permute-done.2, f32[16,128,1]{2,1,0:T(8,128)} %copy.99, f32[16,128,1]{2,1,0:T(8,128)S(1)} %copy.97, f32[256]{0:T(256)S(1)} %copy-done.22, ...), kind=kLoop, calls=%fused_computation.8 | loop fusion | flops 5767168 | bytes 4506624 | tf_op jit(solution)/shard_map/mul | solution.py:151
  25.0 6.3 %all-to-all-start = ((f32[16,128,256]{2,1,0:T(8,128)}), f32[16,128,256]{2,1,0:T(8,128)S(1)}, u32[]{:S(2)}, u32[]{:S(2)}) async-start(f32[16,128,256]{2,1,0:T(8,128)} %fusion.7), calls=%async_computation | async-start | bytes 4194304 | tf_op jit(solution)/shard_map/all_to_all | solution.py:154
  32.6 3.1 %negate_bitcast_fusion = f32[2,16,8,2048]{3,2,1,0:T(8,128)} fusion(f32[2,128,2048]{2,1,0:T(8,128)} %param.13), kind=kLoop, calls=%fused_computation.27 | loop fusion | flops 524288 | bytes 4194304 | tf_op jit(solution)/shard_map/reshape | solution.py:104
  35.7 24.1 %all-to-all-done = f32[16,128,256]{2,1,0:T(8,128)S(1)} async-done(((f32[16,128,256]{2,1,0:T(8,128)}), f32[16,128,256]{2,1,0:T(8,128)S(1)}, u32[]{:S(2)}, u32[]{:S(2)}) %all-to-all-start) | async-done | bytes 2097184 | tf_op jit(solution)/shard_map/all_to_all | solution.py:154
  59.8 2.5 %copy.528 = f32[8,2,128,256]{3,0,2,1:T(8,128)} copy(f32[8,2,128,256]{3,2,1,0:T(8,128)S(1)} %bitcast.656) | data formatting | bytes 4194304 | tf_op jit(solution)/shard_map/all_to_all | solution.py:154
  64.0 17.1 %fusion = f32[2,16,8,2048]{3,2,1,0:T(8,128)S(1)} fusion(f32[2,16,8,2048]{3,2,1,0:T(8,128)S(1)} %dot_general.8, f32[2048,2048]{1,0:T(8,128)} %param.12), kind=kOutput, calls=%fused_computation | convolution fusion | flops 12884901888 | bytes 20971520 | tf_op jit(solution)/shard_map/kji,im->kjm/dot_general | solution.py:152
  81.2 3.2 %fusion.115 = (f32[2,16,1,2048]{3,2,1,0:T(1,128)S(1)}, f32[2,16,1,2048]{3,2,1,0:T(1,128)S(1)}, f32[2,16,1,2048]{3,2,1,0:T(1,128)S(1)}, f32[2,16,1,2048]{3,2,1,0:...) fusion(f32[2,16,8,2048]{3,2,1,0:T(8,128)S(1)} %fusion, ...), kind=kLoop, calls=%fused_computation.395 | loop fusion | bytes 8388608 | tf_op jit(solution)/shard_map/slice | solution.py:116
  85.7 2.2 %fusion.41 = (f32[2,16,2048]{2,0,1:T(2,128)S(1)}, f32[2,16,2048]{2,0,1:T(2,128)S(1)}) fusion(f32[2,16,1,2048]{3,2,1,0:T(1,128)S(1)} %get-tuple-element.89, f32[2,16,1,2048]{3,2,1,0:T(1,128)S(1)} %get-tuple-element.83, f32[2,16,1,2048]{3,2,1,0:T(1,128)S(1)} %get-tuple-element.84, f32[2,16,1,2048]{3,2,1,0:T(1,128)S(1)} %get-tuple-element.85, ...), kind=kLoop, calls=%fused_computation.77 | loop fusion | flops 1441792 | bytes 4456448 | tf_op jit(solution)/shard_map/mul | solution.py:116
  91.1 6.8 %all-to-all-start.1 = ((f32[16,4,2048]{2,1,0:T(4,128)}), f32[16,4,2048]{2,1,0:T(4,128)}, u32[]{:S(2)}, u32[]{:S(2)}) async-start(f32[16,4,2048]{2,1,0:T(4,128)} %broadcast_in_dim.48), calls=%async_computation.1 | async-start | bytes 1048576 | tf_op jit(solution)/shard_map/all_to_all | solution.py:22
  101.0 1.9 constant_dynamic-update-slice_fusion.3
  109.0 4.1 %multiply_add_fusion.1 = (f32[8,4,8,2048]{3,0,1,2:T(8,128)S(1)}, f32[8,4,8,2048]{3,0,1,2:T(8,128)}) fusion(f32[8,4,8,2048]{3,0,1,2:T(8,128)} %bitcast.661, f32[8,4,8,2048]{3,0,1,2:T(8,128)} %bitcast.662, f32[8,4,2048]{2,0,1:T(8,128)S(1)} %bitcast.664, f32[8,4,2048]{2,0,1:T(8,128)S(1)} %bitcast.663), kind=kLoop, calls=%fused_computation.26 | loop fusion | flops 1572864 | bytes 8912896 | tf_op jit(solution)/shard_map/add | solution.py:137
  115.1 4.9 %fusion.16 = (f32[2,16,8,2048]{3,2,1,0:T(8,128)S(1)}, f32[2,16,8,2048]{3,2,1,0:T(8,128)S(1)}) fusion(f32[2,128,2048]{2,1,0:T(8,128)} %param.14, f32[2,16,8,2048]{3,0,1,2:T(2,128)S(1)} %bitcast.655, f32[2,16,8,2048]{3,0,1,2:T(2,128)S(1)} %bitcast.654, f32[2,2048]{1,0:T(2,128)S(1)} %fusion.57, f32[2,128,2048]{2,1,0:T(8,128)} %param.15), kind=kLoop, calls=%fused_computation.21 | loop fusion | flops 2621440 | bytes 12599296 | tf_op jit(solution)/shard_map/reshape | solution.py:105
  123.1 2.4 %bitcast_add_fusion.1 = (f32[2,16,2048]{2,0,1:T(2,128)S(1)}, f32[2,16,2048]{2,0,1:T(2,128)S(1)}) fusion(f32[2,16,1,2048]{3,2,1,0:T(1,128)S(1)} %get-tuple-element.75, f32[2,16,1,2048]{3,2,1,0:T(1,128)S(1)} %get-tuple-element.69, f32[2,16,1,2048]{3,2,1,0:T(1,128)S(1)} %get-tuple-element.70, f32[2,16,1,2048]{3,2,1,0:T(1,128)S(1)} %get-tuple-element.71, ...), kind=kLoop, calls=%fused_computation.53 | loop fusion | flops 1507328 | bytes 4718592 | tf_op jit(solution)/shard_map/add | solution.py:116
  125.9 3.7 %add_dynamic-update-slice_fusion = (f32[2,16,8,2048]{3,0,1,2:T(2,128)}, f32[2,16,1,2048]{3,0,1,2:T(2,128)}, f32[2,16,1,2048]{3,0,1,2:T(2,128)S(1)}, f32[2,16,1,2...) fusion(f32[2,16,1,2048]{3,2,1,0:T(1,128)S(1)} %get-tuple-elemen, ...), kind=kLoop, calls=%fused_computation.101 | loop fusion | flops 1507326 | bytes 6029312
  132.4 5.7 %all-to-all-start.2 = ((f32[16,4,2048]{2,1,0:T(4,128)}), f32[16,4,2048]{2,1,0:T(4,128)}, u32[]{:S(2)}, u32[]{:S(2)}) async-start(f32[16,4,2048]{2,1,0:T(4,128)} %broadcast_in_dim.52), calls=%async_computation.2 | async-start | bytes 1048576 | tf_op jit(solution)/shard_map/all_to_all | solution.py:22
  138.1 2.3 %constant_dynamic-update-slice_fusion.52 = (f32[2,16,8,2048]{3,0,1,2:T(2,128)}, f32[2,16,8,2048]{3,0,1,2:T(2,128)}) fusion(f32[2,16,8,2048]{3,0,1,2:T(2,128)} %get-tuple-element.13, f32[2,16,1,2048]{3,2,1,0:T(1,128)S(1)} %get-tuple-element.69, f32[2,16,1,2048]{3,0,1,2:T(2,128)} %get-tuple-element.14, f32[2,16,1,2048]{3,2,1,0:T(1,128)S(1)} %get-tuple-element.107, ...), kind=kLoop, calls=%fused_computation.169 | loop fusion | flops 196608 | bytes 1572864
  150.1 4.2 %multiply_add_fusion = (f32[8,4,8,2048]{3,0,1,2:T(8,128)S(1)}, f32[8,4,8,2048]{3,0,1,2:T(8,128)}) fusion(f32[8,4,8,2048]{3,0,1,2:T(8,128)} %bitcast.659, f32[8,4,8,2048]{3,0,1,2:T(8,128)} %bitcast.660, f32[8,4,2048]{2,0,1:T(8,128)S(1)} %bitcast.665, f32[8,4,2048]{2,0,1:T(8,128)S(1)} %bitcast.666), kind=kLoop, calls=%fused_computation.25 | loop fusion | flops 1572864 | bytes 8912896 | tf_op jit(solution)/shard_map/add | solution.py:137
  156.3 26.6 %fusion.2 = f32[2,128,2048]{2,1,0:T(8,128)S(1)} fusion(f32[2048,2048]{1,0:T(8,128)} %param.12, f32[2,16,8,2048]{3,0,1,2:T(2,128)S(1)} %bitcast.653, f32[2,16,8,2048]{3,0,1,2:T(2,128)S(1)} %bitcast.652, f32[2,2048]{1,0:T(2,128)S(1)} %fusion.55), kind=kOutput, calls=%fused_computation.2 | convolution fusion | flops 12885950464 | bytes 23085056 | tf_op jit(solution)/shard_map/kjm,im->kji/dot_general | solution.py:168
  183.2 30.9 %all_to_all.30 = f32[8,2,128,256]{3,2,1,0:T(8,128)S(1)} all-to-all(f32[8,2,128,256]{3,2,1,0:T(8,128)S(1)} %fusion.20), channel_id=1, replica_groups=mesh['lat'=16,'lon'=8] {'lon'}, dimensions={0} | all-to-all | bytes 4194304 | tf_op jit(solution)/shard_map/all_to_all | solution.py:170
  (167 shorter events, 43.6 us)
Async XLA Ops:
  1.0 20.0 %collective-permute-start.2 = (f32[16,1,256]{2,1,0:T(1,128)S(1)}, f32[16,1,256]{2,1,0:T(1,128)S(1)}, u32[]{:S(2)}, u32[]{:S(2)}) collective-permute-start(f32[16,1,256]{2,1,0:T(1,128)S(1)} %get-tuple-element.92), channel_id=1, source_target_pairs={{0,8},{8,16},{16,24},{24,32},{32,40},{40,48},{48,56},{56,64},{64,7... | collective-permute-start | bytes 49160 | tf_op jit(solution)/shard_map/ppermute | solution.py:14
  5.9 15.0 %collective-permute-start.3 = (f32[16,1,256]{2,1,0:T(1,128)S(1)}, f32[16,1,256]{2,1,0:T(1,128)S(1)}, u32[]{:S(2)}, u32[]{:S(2)}) collective-permute-start(f32[16,1,256]{2,1,0:T(1,128)S(1)} %get-tuple-element.93), channel_id=1, source_target_pairs={{8,0},{16,8},{24,16},{32,24},{40,32},{48,40},{56,48},{64,56},{72,6... | collective-permute-start | bytes 49160 | tf_op jit(solution)/shard_map/ppermute | solution.py:15
  10.7 10.2 %copy-start.1 = (f32[16,128,256]{2,1,0:T(8,128)S(1)}, f32[16,128,256]{2,1,0:T(8,128)}, u32[]{:S(2)}) copy-start(f32[16,128,256]{2,1,0:T(8,128)} %param.8) | copy-start | bytes 6291460
  10.7 10.2 %copy-start.20 = (f32[128,256]{1,0:T(8,128)S(1)}, f32[128,256]{1,0:T(8,128)}, u32[]{:S(2)}) copy-start(f32[128,256]{1,0:T(8,128)} %param.10) | copy-start | bytes 393220
  10.7 10.2 %copy-start.21 = (f32[128,256]{1,0:T(8,128)S(1)}, f32[128,256]{1,0:T(8,128)}, u32[]{:S(2)}) copy-start(f32[128,256]{1,0:T(8,128)} %param.9) | copy-start | bytes 393220
  10.7 10.3 %copy-start.22 = (f32[256]{0:T(256)S(1)}, f32[256]{0:T(256)}, u32[]{:S(2)}) copy-start(f32[256]{0:T(256)} %param.11) | copy-start | bytes 3076
  12.5 6.3 %collective-permute-start = (f32[16,128,1]{1,0,2:T(8,128)S(1)}, f32[16,128,1]{1,0,2:T(8,128)S(1)}, u32[]{:S(2)}, u32[]{:S(2)}) collective-permute-start(f32[16,128,1]{1,0,2:T(8,128)S(1)} %copy.147), channel_id=1, source_target_pairs={{0,1},{1,2},{2,3},{3,4},{4,5},{5,6},{6,7},{7,0},{8,9},{9,10},{10,1... | collective-permute-start | bytes 24584 | tf_op jit(solution)/shard_map/ppermute | solution.py:14
  15.6 4.0 %collective-permute-start.1 = (f32[16,128,1]{1,0,2:T(8,128)S(1)}, f32[16,128,1]{1,0,2:T(8,128)S(1)}, u32[]{:S(2)}, u32[]{:S(2)}) collective-permute-start(f32[16,128,1]{1,0,2:T(8,128)S(1)} %copy.148), channel_id=1, source_target_pairs={{1,0},{2,1},{3,2},{4,3},{5,4},{6,5},{7,6},{0,7},{9,8},{10,9},{11,1... | collective-permute-start | bytes 24584 | tf_op jit(solution)/shard_map/ppermute | solution.py:15
  25.0 34.8 %all-to-all-start = ((f32[16,128,256]{2,1,0:T(8,128)}), f32[16,128,256]{2,1,0:T(8,128)S(1)}, u32[]{:S(2)}, u32[]{:S(2)}) async-start(f32[16,128,256]{2,1,0:T(8,128)} %fusion.7), calls=%async_computation | async-start | bytes 4194304 | tf_op jit(solution)/shard_map/all_to_all | solution.py:154
  64.0 17.2 %copy-start.3 = (f32[2,16,8,2048]{3,2,1,0:T(8,128)S(1)}, f32[2,16,8,2048]{3,2,1,0:T(8,128)}, u32[]{:S(2)}) copy-start(f32[2,16,8,2048]{3,2,1,0:T(8,128)} %negate_bitcast_fusion) | copy-start | bytes 6291460
  84.5 3.4 %copy-start.4 = (f32[2,16,1,2048]{3,2,1,0:T(1,128)}, f32[2,16,1,2048]{3,2,1,0:T(1,128)S(1)}, u32[]{:S(2)}) copy-start(f32[2,16,1,2048]{3,2,1,0:T(1,128)S(1)} %get-tuple-element.189) | copy-start | bytes 786436
  84.5 3.4 %copy-start.6 = (f32[2,16,1,2048]{3,2,1,0:T(1,128)}, f32[2,16,1,2048]{3,2,1,0:T(1,128)S(1)}, u32[]{:S(2)}) copy-start(f32[2,16,1,2048]{3,2,1,0:T(1,128)S(1)} %get-tuple-element.85) | copy-start | bytes 786436
  84.5 3.4 %copy-start.8 = (f32[2,16,1,2048]{3,2,1,0:T(1,128)}, f32[2,16,1,2048]{3,2,1,0:T(1,128)S(1)}, u32[]{:S(2)}) copy-start(f32[2,16,1,2048]{3,2,1,0:T(1,128)S(1)} %get-tuple-element.186) | copy-start | bytes 786436
  85.7 2.8 %copy-start.13 = (f32[2,16,2048]{2,0,1:T(2,128)S(1)}, f32[2,16,2048]{2,0,1:T(2,128)}, u32[]{:S(2)}) copy-start(f32[2,16,2048]{2,0,1:T(2,128)} %constant_dynamic-update-slice_fusion.29) | copy-start | bytes 786436
  91.1 22.0 %all-to-all-start.1 = ((f32[16,4,2048]{2,1,0:T(4,128)}), f32[16,4,2048]{2,1,0:T(4,128)}, u32[]{:S(2)}, u32[]{:S(2)}) async-start(f32[16,4,2048]{2,1,0:T(4,128)} %broadcast_in_dim.48), calls=%async_computation.1 | async-start | bytes 1048576 | tf_op jit(solution)/shard_map/all_to_all | solution.py:22
  97.9 3.2 %copy-start.7 = (f32[2,16,1,2048]{3,2,1,0:T(1,128)S(1)}, f32[2,16,1,2048]{3,2,1,0:T(1,128)}, u32[]{:S(2)}) copy-start(f32[2,16,1,2048]{3,2,1,0:T(1,128)} %copy-done.6) | copy-start | bytes 786436
  97.9 3.1 %copy-start.9 = (f32[2,16,1,2048]{3,2,1,0:T(1,128)S(1)}, f32[2,16,1,2048]{3,2,1,0:T(1,128)}, u32[]{:S(2)}) copy-start(f32[2,16,1,2048]{3,2,1,0:T(1,128)} %copy-done.8) | copy-start | bytes 786436
  104.3 3.1 %copy-start.5 = (f32[2,16,1,2048]{3,2,1,0:T(1,128)S(1)}, f32[2,16,1,2048]{3,2,1,0:T(1,128)}, u32[]{:S(2)}) copy-start(f32[2,16,1,2048]{3,2,1,0:T(1,128)} %copy-done.4) | copy-start | bytes 786436
  106.0 2.9 %copy-start.12 = (f32[2,16,2048]{2,0,1:T(2,128)S(1)}, f32[2,16,2048]{2,0,1:T(2,128)}, u32[]{:S(2)}) copy-start(f32[2,16,2048]{2,0,1:T(2,128)} %copy-done.11) | copy-start | bytes 786436
  106.0 2.9 %copy-start.15 = (f32[2,16,2048]{2,0,1:T(2,128)S(1)}, f32[2,16,2048]{2,0,1:T(2,128)}, u32[]{:S(2)}) copy-start(f32[2,16,2048]{2,0,1:T(2,128)} %copy-done.14) | copy-start | bytes 786436
  132.4 21.9 %all-to-all-start.2 = ((f32[16,4,2048]{2,1,0:T(4,128)}), f32[16,4,2048]{2,1,0:T(4,128)}, u32[]{:S(2)}, u32[]{:S(2)}) async-start(f32[16,4,2048]{2,1,0:T(4,128)} %broadcast_in_dim.52), calls=%async_computation.2 | async-start | bytes 1048576 | tf_op jit(solution)/shard_map/all_to_all | solution.py:22
  145.6 4.5 %copy-start.17 = (f32[2,16,2048]{2,0,1:T(2,128)S(1)}, f32[2,16,2048]{2,0,1:T(2,128)}, u32[]{:S(2)}) copy-start(f32[2,16,2048]{2,0,1:T(2,128)} %copy-done.16) | copy-start | bytes 786436
  145.6 4.5 %copy-start.19 = (f32[2,16,2048]{2,0,1:T(2,128)S(1)}, f32[2,16,2048]{2,0,1:T(2,128)}, u32[]{:S(2)}) copy-start(f32[2,16,2048]{2,0,1:T(2,128)} %copy-done.18) | copy-start | bytes 786436
  154.3 2.1 copy-start
  (6 other events, 6.4 us)
